TPU v7x, 32 devices: a whole 2x2x4 slice. The times are simulated.
32 devices in a mesh: frame: 4 (over x, core), within: 8 (over z, y).
Axes of the slice: x: 2, y: 2, z: 4, core: 2. Of those that a mesh axis runs over, the one named last changes fastest.
Arguments:
- queries: bfloat16 [4, 576, 1024], P('frame', 'within'), may hold values from -6 to 6
- keys_in: bfloat16 [4, 576, 1024], P('frame', 'within'), may hold values from -6 to 6
- values_in: bfloat16 [4, 576, 1024], P('frame', 'within'), may hold values from -6 to 6
- grad_out: bfloat16 [4, 576, 1024], P('frame', 'within'), may hold values from -6 to 6
- partners: int32 [4, 2], replicated, may hold values from 0 to 3
- registers: int32 [4], replicated, may hold values from 1 to 144
Outputs:
- grad_queries: bfloat16 [4, 576, 1024], P('frame', 'within')
- grad_keys: bfloat16 [4, 576, 1024], P('frame', 'within')
- grad_values: bfloat16 [4, 576, 1024], P('frame', 'within')
Inputs may be any that keep to these rules, and one draw needn't show every extreme that they name: `partners`: A row may list a group more than once, and may list its own group.
All inputs are finite; a program needn't handle non-finite values.
Results may differ from a plain program's by a relative error of at most 0.012.
Values may be sent and summed in bfloat16 or wider, within the bound.
A program may use at most 128 MiB of HBM per device.

v0:
```python
import jax
import jax.numpy as jnp
from jax import lax
from jax.sharding import PartitionSpec as P

DH = 64


def local(queries, keys_in, values_in, grad_out, partners, registers):
    q_wide, k_wide, v_wide, d_wide = (
        lax.all_to_all(queries, "within", split_axis=2, concat_axis=1, tiled=True),
        lax.all_to_all(keys_in, "within", split_axis=2, concat_axis=1, tiled=True),
        lax.all_to_all(values_in, "within", split_axis=2, concat_axis=1, tiled=True),
        lax.all_to_all(grad_out, "within", split_axis=2, concat_axis=1, tiled=True),
    )
    seq = q_wide.shape[1]
    cols = q_wide.shape[2]
    heads_here = cols // DH
    scale = DH ** (-0.5)

    def split_heads(block):
        return block.reshape(seq, heads_here, DH)

    query3 = split_heads(q_wide[0])
    key3 = split_heads(k_wide[0])
    value3 = split_heads(v_wide[0])
    cotan3 = split_heads(d_wide[0])
    group = lax.axis_index("frame")
    listed = partners[group]
    positions = jnp.arange(seq, dtype=jnp.int32)
    everyone = jnp.ones((seq,), jnp.float32)
    groups = lax.axis_size("frame") * queries.shape[0]

    def patches(other):
        return (positions >= registers[other]).astype(jnp.float32)

    def logits(keys_here, visible):
        raw = (
            jnp.einsum("qhd,khd->hqk", query3, keys_here, preferred_element_type=jnp.float32)
            * scale
        )
        return jnp.where(visible[None, None, :] > 0, raw, -1e30)

    def stats(state, keys_here, values_here, visible, weight):
        old_top, old_total, old_dsum = state
        raw = logits(keys_here, visible)
        top = jnp.max(raw, axis=2)
        expo = jnp.exp(raw - top[:, :, None])
        dprod = jnp.einsum("qhd,khd->hqk", cotan3, values_here, preferred_element_type=jnp.float32)
        total = weight * jnp.sum(expo, axis=2)
        dsum = weight * jnp.sum(expo * dprod, axis=2)
        new_top = jnp.maximum(old_top, top)
        keep_old = jnp.exp(old_top - new_top)
        keep_new = jnp.exp(top - new_top)
        return (
            new_top,
            old_total * keep_old + total * keep_new,
            old_dsum * keep_old + dsum * keep_new,
        )

    def grads(final, keys_here, values_here, visible, weight):
        top, total, delta = final
        raw = logits(keys_here, visible)
        prob = jnp.exp(raw - top[:, :, None]) / total[:, :, None]
        dprod = jnp.einsum("qhd,khd->hqk", cotan3, values_here, preferred_element_type=jnp.float32)
        dscore = prob * (dprod - delta[:, :, None])
        dscore_low = dscore.astype(jnp.bfloat16)
        dq_add = jnp.einsum(
            "hqk,khd->qhd", dscore_low, keys_here, preferred_element_type=jnp.float32
        ) * (scale * weight)
        prob_low = prob.astype(jnp.bfloat16)
        dk_add = jnp.einsum(
            "hqk,qhd->khd", dscore_low, query3, preferred_element_type=jnp.float32
        ) * (scale * weight)
        dv_add = (
            jnp.einsum("hqk,qhd->khd", prob_low, cotan3, preferred_element_type=jnp.float32)
            * weight
        )
        return (dq_add.reshape(seq, cols), dk_add.reshape(seq, cols), dv_add.reshape(seq, cols))

    blank = jnp.zeros((heads_here, seq), jnp.float32)
    state = stats((blank - 1e30, blank, blank), key3, value3, everyone, 1.0)
    keys_all, values_all = (
        lax.all_gather(k_wide, "frame", axis=0, tiled=True),
        lax.all_gather(v_wide, "frame", axis=0, tiled=True),
    )
    for slot in range(listed.shape[0]):
        other = listed[slot]
        state = stats(
            state, split_heads(keys_all[other]), split_heads(values_all[other]), patches(other), 1.0
        )
    top, total, dsum = state
    final = (top, total, dsum / total)
    own_terms = grads(final, key3, value3, everyone, 1.0)
    empty = jnp.zeros((groups, seq, cols), jnp.float32)
    results = (own_terms[0], empty.at[group].add(own_terms[1]), empty.at[group].add(own_terms[2]))
    for slot in range(listed.shape[0]):
        other = listed[slot]
        added = grads(
            final, split_heads(keys_all[other]), split_heads(values_all[other]), patches(other), 1.0
        )
        results = (
            results[0] + added[0],
            results[1].at[other].add(added[1]),
            results[2].at[other].add(added[2]),
        )
    dq_sum = results[0]
    got_keys, got_values = (
        lax.all_to_all(results[1], "frame", split_axis=0, concat_axis=0, tiled=True),
        lax.all_to_all(results[2], "frame", split_axis=0, concat_axis=0, tiled=True),
    )
    dk_mine = jnp.sum(got_keys, axis=0, keepdims=True)
    dv_mine = jnp.sum(got_values, axis=0, keepdims=True)
    dq_low = dq_sum.astype(jnp.bfloat16)[None]
    dk_low = dk_mine.astype(jnp.bfloat16)
    dv_low = dv_mine.astype(jnp.bfloat16)
    return (
        lax.all_to_all(dq_low, "within", split_axis=1, concat_axis=2, tiled=True),
        lax.all_to_all(dk_low, "within", split_axis=1, concat_axis=2, tiled=True),
        lax.all_to_all(dv_low, "within", split_axis=1, concat_axis=2, tiled=True),
    )


def solution(mesh):
    placed = (
        P("frame", "within", None),
        P("frame", "within", None),
        P("frame", "within", None),
        P("frame", "within", None),
        P(),
        P(),
    )
    return jax.shard_map(
        local,
        mesh=mesh,
        in_specs=placed,
        out_specs=(
            P("frame", "within", None),
            P("frame", "within", None),
            P("frame", "within", None),
        ),
        check_vma=False,
    )
```

profile of v0, /device:TPU:0, one launch (start us, length us, event | category | flops | bytes accessed | tf_op | source)
XLA Modules:
  0.0 192.7 jit_solution(5798555888546599513)
XLA Ops:
  2.5 2.4 %reduce.31 = bf16[1024,72]{1,0:T(8,128)(2,1)S(1)} reduce(bf16[1024,1,72]{2,1,0:T(2,128)(2,1)S(1)} %bitcast.216, bf16[]{:T(256)} %broadcast.248), dimensions={1}, to_apply=%bitcast.168.reduce_sub_computation | reduce | bytes 294914
  6.1 7.3 %all-to-all-start.1 = ((bf16[8,2,4608]{2,1,0:T(2,128)(2,1)}), bf16[8,2,4608]{2,1,0:T(2,128)(2,1)S(1)}, u32[]{:S(2)}, u32[]{:S(2)}) async-start(bf16[8,2,4608]{2,1,0:T(2,128)(2,1)} %reshape.379), calls=%async_computation.1 | async-start | bytes 294912 | tf_op jit(solution)/shard_map/all_to_all | solution.py:12
  18.0 2.4 %reduce.30 = bf16[1024,72]{1,0:T(8,128)(2,1)S(1)} reduce(bf16[1024,1,72]{2,1,0:T(2,128)(2,1)S(1)} %bitcast.221, bf16[]{:T(256)} %broadcast.248), dimensions={1}, to_apply=%bitcast.170.reduce_sub_computation | reduce | bytes 294914
  24.3 6.0 %all-to-all-start.3 = ((bf16[8,2,4608]{2,1,0:T(2,128)(2,1)}), bf16[8,2,4608]{2,1,0:T(2,128)(2,1)S(1)}, u32[]{:S(2)}, u32[]{:S(2)}) async-start(bf16[8,2,4608]{2,1,0:T(2,128)(2,1)} %reshape.381), calls=%async_computation.3 | async-start | bytes 294912 | tf_op jit(solution)/shard_map/all_to_all | solution.py:13
  32.1 2.4 %reduce.32 = bf16[1024,72]{1,0:T(8,128)(2,1)S(1)} reduce(bf16[1024,1,72]{2,1,0:T(2,128)(2,1)S(1)} %bitcast.222, bf16[]{:T(256)} %broadcast.248), dimensions={1}, to_apply=%bitcast.174.reduce_sub_computation | reduce | bytes 294914
  36.0 2.4 %reduce.33 = bf16[1024,72]{1,0:T(8,128)(2,1)S(1)} reduce(bf16[1024,1,72]{2,1,0:T(2,128)(2,1)S(1)} %bitcast.223, bf16[]{:T(256)} %broadcast.248), dimensions={1}, to_apply=%bitcast.172.reduce_sub_computation | reduce | bytes 294914
  40.9 6.0 %all-to-all-start = ((bf16[8,2,4608]{2,1,0:T(2,128)(2,1)}), bf16[8,2,4608]{2,1,0:T(2,128)(2,1)S(1)}, u32[]{:S(2)}, u32[]{:S(2)}) async-start(bf16[8,2,4608]{2,1,0:T(2,128)(2,1)} %reshape.385), calls=%async_computation | async-start | bytes 294912 | tf_op jit(solution)/shard_map/all_to_all | solution.py:11
  48.2 7.5 %all_gather.6 = bf16[4,576,128]{2,1,0:T(8,128)(2,1)S(1)} all-gather(bf16[1,576,128]{2,1,0:T(8,128)(2,1)S(1)} %bitcast.249), channel_id=1, replica_groups=mesh['frame'=4,'within'=8] {'frame'}, dimensions={0}, use_global_device_ids=true | all-gather | bytes 737280 | tf_op jit(solution)/shard_map/all_gather | solution.py:84
  55.8 7.6 %all_gather.7 = bf16[4,576,128]{2,1,0:T(8,128)(2,1)S(1)} all-gather(bf16[1,576,128]{2,1,0:T(8,128)(2,1)S(1)} %bitcast.254), channel_id=1, replica_groups=mesh['frame'=4,'within'=8] {'frame'}, dimensions={0}, use_global_device_ids=true | all-gather | bytes 737280 | tf_op jit(solution)/shard_map/all_gather | solution.py:85
  63.4 6.0 %all-to-all-start.2 = ((bf16[8,2,4608]{2,1,0:T(2,128)(2,1)}), bf16[8,2,4608]{2,1,0:T(2,128)(2,1)S(1)}, u32[]{:S(2)}, u32[]{:S(2)}) async-start(bf16[8,2,4608]{2,1,0:T(2,128)(2,1)} %reshape.383), calls=%async_computation.2 | async-start | bytes 294912 | tf_op jit(solution)/shard_map/all_to_all | solution.py:14
  73.3 3.9 %all-to-all-done.2 = bf16[8,2,4608]{2,1,0:T(2,128)(2,1)S(1)} async-done(((bf16[8,2,4608]{2,1,0:T(2,128)(2,1)}), bf16[8,2,4608]{2,1,0:T(2,128)(2,1)S(1)}, u32[]{:S(2)}, u32[]{:S(2)}) %all-to-all-start.2) | async-done | bytes 147488 | tf_op jit(solution)/shard_map/all_to_all | solution.py:14
  85.5 2.8 %fusion.14 = (f32[2,576]{1,0:T(2,128)S(1)}, f32[2,576]{1,0:T(2,128)S(1)}, f32[2,576,576]{2,1,0:T(8,128)}) fusion(f32[2,576,576]{2,1,0:T(8,128)S(1)} %get-tuple-element.99, f32[2,576]{1,0:T(2,128)S(1)} %get-tuple-element.98, pred[576]{0:T(1024)(128)(4,1)S(1)} %get-tuple-element.109, bf16[576,2,64]{0,2,1:T(8,128)(2,1)S(1)} %bitcast.238, ...), kind=kOutput, calls=%fused_computation.30 | convolution fusion | flops 88913664 | bytes 5617728 | tf_op jit(solution)/shard_map/qhd,khd->hqk/dot_general | solution.py:49
  88.3 2.8 %fusion.13 = (f32[2,576]{1,0:T(2,128)S(1)}, f32[2,576]{1,0:T(2,128)S(1)}, f32[2,576,576]{2,1,0:T(8,128)}) fusion(f32[2,576,576]{2,1,0:T(8,128)S(1)} %get-tuple-element.102, f32[2,576]{1,0:T(2,128)S(1)} %get-tuple-element.101, pred[576]{0:T(1024)(128)(4,1)S(1)} %get-tuple-element.110, bf16[576,2,64]{0,2,1:T(8,128)(2,1)S(1)} %bitcast.239, ...), kind=kOutput, calls=%fused_computation.29 | convolution fusion | flops 88913664 | bytes 5617728 | tf_op jit(solution)/shard_map/qhd,khd->hqk/dot_general | solution.py:49
  91.0 2.5 %fusion.12 = (f32[2,576]{1,0:T(2,128)S(1)}, f32[2,576]{1,0:T(2,128)S(1)}, f32[2,576,576]{1,2,0:T(8,128)}) fusion(f32[2,576,576]{1,2,0:T(8,128)S(1)} %get-tuple-element.105, f32[2,576]{1,0:T(2,128)S(1)} %get-tuple-element.104, bf16[576,2,64]{0,2,1:T(8,128)(2,1)S(1)} %reshape_squeeze.32, bf16[576,2,64]{0,2,1:T(8,128)(2,1)S(1)} %copy-done.14), kind=kOutput, calls=%fused_computation.28 | convolution fusion | flops 88250112 | bytes 5617152 | tf_op jit(solution)/shard_map/qhd,khd->hqk/dot_general | solution.py:65
  97.0 1.8 copy.145
  98.8 1.8 copy.143
  100.6 2.0 %fusion.27 = f32[2,576,64]{1,2,0:T(8,128)} fusion(bf16[576,2,64]{0,2,1:T(8,128)(2,1)S(1)} %reshape_squeeze.32, f32[2,576,576]{1,2,0:T(8,128)S(1)} %get-tuple-element.105, f32[2,576]{1,0:T(2,128)S(1)} %get-tuple-element.87, f32[2,576]{1,0:T(2,128)S(1)} %get-tuple-element.92, pred[]{:T(512)} %get-tuple-element.95), kind=kOutput, calls=%fused_computation.50 | convolution fusion | flops 87662592 | bytes 3105793 | tf_op jit(solution)/shard_map/hqk,qhd->khd/dot_general | solution.py:76
  102.7 1.8 copy.141
  104.5 7.0 %fusion.5 = (bf16[2,576,576]{1,2,0:T(8,128)(2,1)S(1)}, bf16[2,576,576]{1,2,0:T(8,128)(2,1)S(1)}, bf16[2,576,576]{1,2,0:T(8,128)(2,1)S(1)}) fusion(f32[2,576,576]{2,1,0:T(8,128)} %get-tuple-element.103, f32[2,576]{1,0:T(2,128)S(1)} %get-tuple-element.88, f32[2,576]{1,0:T(2,128)S(1)} %get-tuple-element.87, f32[2,576]{1,0:T(2,128)S(1)} %get-tuple-element.92, ...), kind=kLoop, calls=%fused_computation.9 | loop fusion | flops 13271040 | bytes 19921536 | tf_op jit(solution)/shard_map/convert_element_type | solution.py:67
  116.1 4.0 %all-to-all-start.4 = ((bf16[8,2,4608]{2,1,0:T(2,128)(2,1)}), bf16[8,2,4608]{2,1,0:T(2,128)(2,1)}, u32[]{:S(2)}, u32[]{:S(2)}) async-start(bf16[8,2,4608]{2,1,0:T(2,128)(2,1)} %reshape.387), calls=%async_computation.4 | async-start | bytes 294912 | tf_op jit(solution)/shard_map/all_to_all | solution.py:118
  121.9 2.5 %fusion.33 = f32[4,576,128]{2,1,0:T(8,128)} fusion(f32[4,576,128]{2,1,0:T(8,128)} %constant_dynamic-update-slice_fusion, s32[]{:T(128)} %select_n.49, f32[1,576,128]{2,1,0:T(8,128)} %copy.143, pred[]{:T(512)} %get-tuple-element.82), kind=kLoop, calls=%fused_computation.58 | loop fusion | flops 147456 | bytes 885760 | tf_op jit(solution)/shard_map/scatter-add | solution.py:105
  124.5 2.4 %fusion.34 = f32[4,576,128]{2,1,0:T(8,128)} fusion(f32[4,576,128]{2,1,0:T(8,128)} %fusion.33, s32[]{:T(128)} %select_n.52, f32[1,576,128]{2,1,0:T(8,128)S(1)} %copy-done.12, pred[]{:T(512)} %get-tuple-element.81), kind=kLoop, calls=%fused_computation.59 | loop fusion | flops 147456 | bytes 885760 | tf_op jit(solution)/shard_map/scatter-add | solution.py:105
  128.0 4.4 %all-to-all-start.7 = ((f32[4,576,128]{2,1,0:T(8,128)}), f32[4,576,128]{2,1,0:T(8,128)}, u32[]{:S(2)}, u32[]{:S(2)}) async-start(f32[4,576,128]{2,1,0:T(8,128)} %fusion.34), calls=%async_computation.7 | async-start | bytes 2359296 | tf_op jit(solution)/shard_map/all_to_all | solution.py:110
  137.6 2.3 %fusion.31 = f32[4,576,128]{2,1,0:T(8,128)} fusion(f32[4,576,128]{2,1,0:T(8,128)} %constant_dynamic-update-slice_fusion.1, s32[]{:T(128)} %select_n.49, f32[1,576,128]{2,1,0:T(8,128)S(1)} %copy.134, pred[]{:T(512)} %get-tuple-element.82), kind=kLoop, calls=%fused_computation.56 | loop fusion | flops 147456 | bytes 885760 | tf_op jit(solution)/shard_map/scatter-add | solution.py:104
  139.9 2.4 %fusion.32 = f32[4,576,128]{2,1,0:T(8,128)} fusion(f32[4,576,128]{2,1,0:T(8,128)} %fusion.31, s32[]{:T(128)} %select_n.52, f32[1,576,128]{2,1,0:T(8,128)S(1)} %copy.136, pred[]{:T(512)} %get-tuple-element.81), kind=kLoop, calls=%fused_computation.57 | loop fusion | flops 147456 | bytes 885760 | tf_op jit(solution)/shard_map/scatter-add | solution.py:104
  142.3 6.1 %all-to-all-done.7 = f32[4,576,128]{2,1,0:T(8,128)} async-done(((f32[4,576,128]{2,1,0:T(8,128)}), f32[4,576,128]{2,1,0:T(8,128)}, u32[]{:S(2)}, u32[]{:S(2)}) %all-to-all-start.7) | async-done | bytes 1179680 | tf_op jit(solution)/shard_map/all_to_all | solution.py:110
  148.3 3.5 %all-to-all-start.5 = ((f32[4,576,128]{2,1,0:T(8,128)}), f32[4,576,128]{2,1,0:T(8,128)S(1)}, u32[]{:S(2)}, u32[]{:S(2)}) async-start(f32[4,576,128]{2,1,0:T(8,128)} %fusion.32), calls=%async_computation.5 | async-start | bytes 2359296 | tf_op jit(solution)/shard_map/all_to_all | solution.py:109
  155.8 11.9 %all-to-all-done.5 = f32[4,576,128]{2,1,0:T(8,128)S(1)} async-done(((f32[4,576,128]{2,1,0:T(8,128)}), f32[4,576,128]{2,1,0:T(8,128)S(1)}, u32[]{:S(2)}, u32[]{:S(2)}) %all-to-all-start.5) | async-done | bytes 1179680 | tf_op jit(solution)/shard_map/all_to_all | solution.py:109
  167.7 5.9 %all-to-all-start.8 = ((bf16[8,2,4608]{2,1,0:T(2,128)(2,1)}), bf16[8,2,4608]{2,1,0:T(2,128)(2,1)S(1)}, u32[]{:S(2)}, u32[]{:S(2)}) async-start(bf16[8,2,4608]{2,1,0:T(2,128)(2,1)} %reshape.391), calls=%async_computation.8 | async-start | bytes 294912 | tf_op jit(solution)/shard_map/all_to_all | solution.py:120
  176.3 4.8 %all-to-all-done.8 = bf16[8,2,4608]{2,1,0:T(2,128)(2,1)S(1)} async-done(((bf16[8,2,4608]{2,1,0:T(2,128)(2,1)}), bf16[8,2,4608]{2,1,0:T(2,128)(2,1)S(1)}, u32[]{:S(2)}, u32[]{:S(2)}) %all-to-all-start.8) | async-done | bytes 147488 | tf_op jit(solution)/shard_map/all_to_all | solution.py:120
  181.0 3.4 %all-to-all-start.6 = ((bf16[8,2,4608]{2,1,0:T(2,128)(2,1)}), bf16[8,2,4608]{2,1,0:T(2,128)(2,1)S(1)}, u32[]{:S(2)}, u32[]{:S(2)}) async-start(bf16[8,2,4608]{2,1,0:T(2,128)(2,1)} %reshape.389), calls=%async_computation.6 | async-start | bytes 294912 | tf_op jit(solution)/shard_map/all_to_all | solution.py:119
  187.4 4.4 %all-to-all-done.6 = bf16[8,2,4608]{2,1,0:T(2,128)(2,1)S(1)} async-done(((bf16[8,2,4608]{2,1,0:T(2,128)(2,1)}), bf16[8,2,4608]{2,1,0:T(2,128)(2,1)S(1)}, u32[]{:S(2)}, u32[]{:S(2)}) %all-to-all-start.6) | async-done | bytes 147488 | tf_op jit(solution)/shard_map/all_to_all | solution.py:119
  (130 shorter events, 52.9 us)
Async XLA Ops:
  0.6 12.7 %copy-start = (s32[4,2]{0,1:T(2,128)S(1)}, s32[4,2]{0,1:T(2,128)}, u32[]{:S(2)}) copy-start(s32[4,2]{0,1:T(2,128)} %param.22) | copy-start | bytes 100
  0.6 22.9 %copy-start.19 = (s32[3]{0:T(128)S(1)}, s32[3]{0:T(128)}, u32[]{:S(2)}) copy-start(s32[3]{0:T(128)} %constant.142.clone.1) | copy-start | bytes 40
  0.7 22.2 %copy-start.18 = (s32[4]{0:T(128)S(1)}, s32[4]{0:T(128)}, u32[]{:S(2)}) copy-start(s32[4]{0:T(128)} %param.23) | copy-start | bytes 52
  0.7 31.0 %copy-start.16 = (bf16[1,72,1024]{2,1,0:T(8,128)(2,1)S(1)}, bf16[1,72,1024]{2,1,0:T(8,128)(2,1)}, u32[]{:S(2)}) copy-start(bf16[1,72,1024]{2,1,0:T(8,128)(2,1)} %param.18) | copy-start | bytes 442372
  2.0 33.7 %copy-start.17 = (bf16[1,72,1024]{2,1,0:T(8,128)(2,1)S(1)}, bf16[1,72,1024]{2,1,0:T(8,128)(2,1)}, u32[]{:S(2)}) copy-start(bf16[1,72,1024]{2,1,0:T(8,128)(2,1)} %param.21) | copy-start | bytes 442372
  6.1 18.3 %all-to-all-start.1 = ((bf16[8,2,4608]{2,1,0:T(2,128)(2,1)}), bf16[8,2,4608]{2,1,0:T(2,128)(2,1)S(1)}, u32[]{:S(2)}, u32[]{:S(2)}) async-start(bf16[8,2,4608]{2,1,0:T(2,128)(2,1)} %reshape.379), calls=%async_computation.1 | async-start | bytes 294912 | tf_op jit(solution)/shard_map/all_to_all | solution.py:12
  24.3 16.6 %all-to-all-start.3 = ((bf16[8,2,4608]{2,1,0:T(2,128)(2,1)}), bf16[8,2,4608]{2,1,0:T(2,128)(2,1)S(1)}, u32[]{:S(2)}, u32[]{:S(2)}) async-start(bf16[8,2,4608]{2,1,0:T(2,128)(2,1)} %reshape.381), calls=%async_computation.3 | async-start | bytes 294912 | tf_op jit(solution)/shard_map/all_to_all | solution.py:13
  40.9 22.5 %all-to-all-start = ((bf16[8,2,4608]{2,1,0:T(2,128)(2,1)}), bf16[8,2,4608]{2,1,0:T(2,128)(2,1)S(1)}, u32[]{:S(2)}, u32[]{:S(2)}) async-start(bf16[8,2,4608]{2,1,0:T(2,128)(2,1)} %reshape.385), calls=%async_computation | async-start | bytes 294912 | tf_op jit(solution)/shard_map/all_to_all | solution.py:11
  63.4 13.7 %all-to-all-start.2 = ((bf16[8,2,4608]{2,1,0:T(2,128)(2,1)}), bf16[8,2,4608]{2,1,0:T(2,128)(2,1)S(1)}, u32[]{:S(2)}, u32[]{:S(2)}) async-start(bf16[8,2,4608]{2,1,0:T(2,128)(2,1)} %reshape.383), calls=%async_computation.2 | async-start | bytes 294912 | tf_op jit(solution)/shard_map/all_to_all | solution.py:14
  83.1 2.4 %copy-start.13 = (bf16[1,576,128]{1,2,0:T(8,128)(2,1)S(1)}, bf16[1,576,128]{1,2,0:T(8,128)(2,1)}, u32[]{:S(2)}) copy-start(bf16[1,576,128]{1,2,0:T(8,128)(2,1)} %copy.125) | copy-start | bytes 442372
  84.8 8.8 %copy-start.1 = (f32[2,576,576]{2,1,0:T(8,128)}, f32[2,576,576]{2,1,0:T(8,128)S(1)}, u32[]{:S(2)}) copy-start(f32[2,576,576]{2,1,0:T(8,128)S(1)} %get-tuple-element.99) | copy-start | bytes 7962628
  85.5 9.8 %copy-start.2 = (f32[2,576,576]{2,1,0:T(8,128)}, f32[2,576,576]{2,1,0:T(8,128)S(1)}, u32[]{:S(2)}) copy-start(f32[2,576,576]{2,1,0:T(8,128)S(1)} %get-tuple-element.102) | copy-start | bytes 7962628
  85.5 2.8 %copy-start.15 = (bf16[1,576,128]{1,2,0:T(8,128)(2,1)S(1)}, bf16[1,576,128]{1,2,0:T(8,128)(2,1)}, u32[]{:S(2)}) copy-start(bf16[1,576,128]{1,2,0:T(8,128)(2,1)} %copy.124) | copy-start | bytes 442372
  88.3 2.8 %copy-start.14 = (bf16[576,2,64]{0,2,1:T(8,128)(2,1)S(1)}, bf16[576,2,64]{0,2,1:T(8,128)(2,1)}, u32[]{:S(2)}) copy-start(bf16[576,2,64]{0,2,1:T(8,128)(2,1)} %reshape_squeeze.33) | copy-start | bytes 442372
  104.5 7.0 %copy-start.10 = (bf16[576,2,64]{0,2,1:T(8,128)(2,1)S(1)}, bf16[576,2,64]{0,2,1:T(8,128)(2,1)}, u32[]{:S(2)}) copy-start(bf16[576,2,64]{0,2,1:T(8,128)(2,1)} %reshape_squeeze.29) | copy-start | bytes 442372
  104.5 7.4 %copy-start.9 = (bf16[1,576,128]{1,2,0:T(8,128)(2,1)S(1)}, bf16[1,576,128]{1,2,0:T(8,128)(2,1)}, u32[]{:S(2)}) copy-start(bf16[1,576,128]{1,2,0:T(8,128)(2,1)} %copy.116) | copy-start | bytes 442372
  111.5 1.2 copy-start.3
  111.5 1.6 copy-start.5
  111.6 2.0 %copy-start.7 = (bf16[2,576,576]{1,2,0:T(8,128)(2,1)}, bf16[2,576,576]{1,2,0:T(8,128)(2,1)S(1)}, u32[]{:S(2)}) copy-start(bf16[2,576,576]{1,2,0:T(8,128)(2,1)S(1)} %get-tuple-element.91) | copy-start | bytes 3981316
  112.4 8.8 %copy-start.11 = (f32[1,576,128]{2,1,0:T(8,128)S(1)}, f32[1,576,128]{2,1,0:T(8,128)}, u32[]{:S(2)}) copy-start(f32[1,576,128]{2,1,0:T(8,128)} %copy.141) | copy-start | bytes 884740
  113.5 10.9 %copy-start.12 = (f32[1,576,128]{2,1,0:T(8,128)S(1)}, f32[1,576,128]{2,1,0:T(8,128)}, u32[]{:S(2)}) copy-start(f32[1,576,128]{2,1,0:T(8,128)} %copy.145) | copy-start | bytes 884740
  113.5 13.3 %copy-start.8 = (bf16[2,576,576]{1,2,0:T(8,128)(2,1)S(1)}, bf16[2,576,576]{1,2,0:T(8,128)(2,1)}, u32[]{:S(2)}) copy-start(bf16[2,576,576]{1,2,0:T(8,128)(2,1)} %copy-done.7) | copy-start | bytes 3981316
  116.1 11.9 %all-to-all-start.4 = ((bf16[8,2,4608]{2,1,0:T(2,128)(2,1)}), bf16[8,2,4608]{2,1,0:T(2,128)(2,1)}, u32[]{:S(2)}, u32[]{:S(2)}) async-start(bf16[8,2,4608]{2,1,0:T(2,128)(2,1)} %reshape.387), calls=%async_computation.4 | async-start | bytes 294912 | tf_op jit(solution)/shard_map/all_to_all | solution.py:118
  121.9 10.5 %copy-start.4 = (bf16[2,576,576]{1,2,0:T(8,128)(2,1)S(1)}, bf16[2,576,576]{1,2,0:T(8,128)(2,1)}, u32[]{:S(2)}) copy-start(bf16[2,576,576]{1,2,0:T(8,128)(2,1)} %copy-done.3) | copy-start | bytes 3981316
  128.0 7.0 %copy-start.6 = (bf16[2,576,576]{1,2,0:T(8,128)(2,1)S(1)}, bf16[2,576,576]{1,2,0:T(8,128)(2,1)}, u32[]{:S(2)}) copy-start(bf16[2,576,576]{1,2,0:T(8,128)(2,1)} %copy-done.5) | copy-start | bytes 3981316
  128.0 20.3 %all-to-all-start.7 = ((f32[4,576,128]{2,1,0:T(8,128)}), f32[4,576,128]{2,1,0:T(8,128)}, u32[]{:S(2)}, u32[]{:S(2)}) async-start(f32[4,576,128]{2,1,0:T(8,128)} %fusion.34), calls=%async_computation.7 | async-start | bytes 2359296 | tf_op jit(solution)/shard_map/all_to_all | solution.py:110
  148.3 19.3 %all-to-all-start.5 = ((f32[4,576,128]{2,1,0:T(8,128)}), f32[4,576,128]{2,1,0:T(8,128)S(1)}, u32[]{:S(2)}, u32[]{:S(2)}) async-start(f32[4,576,128]{2,1,0:T(8,128)} %fusion.32), calls=%async_computation.5 | async-start | bytes 2359296 | tf_op jit(solution)/shard_map/all_to_all | solution.py:109
  167.7 13.4 %all-to-all-start.8 = ((bf16[8,2,4608]{2,1,0:T(2,128)(2,1)}), bf16[8,2,4608]{2,1,0:T(2,128)(2,1)S(1)}, u32[]{:S(2)}, u32[]{:S(2)}) async-start(bf16[8,2,4608]{2,1,0:T(2,128)(2,1)} %reshape.391), calls=%async_computation.8 | async-start | bytes 294912 | tf_op jit(solution)/shard_map/all_to_all | solution.py:120
  181.0 10.8 %all-to-all-start.6 = ((bf16[8,2,4608]{2,1,0:T(2,128)(2,1)}), bf16[8,2,4608]{2,1,0:T(2,128)(2,1)S(1)}, u32[]{:S(2)}, u32[]{:S(2)}) async-start(bf16[8,2,4608]{2,1,0:T(2,128)(2,1)} %reshape.389), calls=%async_computation.6 | async-start | bytes 294912 | tf_op jit(solution)/shard_map/all_to_all | solution.py:119
where the time goes:
time: 194 us; the launch traced here: 193 us
  starting transfers between devices  46.5 us (24%)
  local copies, waits for them, and re-layouts  38.9 us (20%)
  other arithmetic  34.3 us (18%)
  waiting for transfers between devices  31 us (16%)
  matrix products  21.4 us (11%)
  blocking collectives  15.2 us (8%)
  between operations  5.28 us (3%)
    unnamed x68, local copies, waits for them, and re-layouts  17.3 us
    unnamed x7, other arithmetic  14.1 us
    all_to_all x1, waiting for transfers between devices, local(): lax.all_to_all(results[1], 'frame', split_axis=0, concat_axis=0, tiled=True)  11.9 us
    all_gather x1, blocking collectives, local(): lax.all_gather(v_wide, 'frame', axis=0, tiled=True)  7.64 us
    all_gather x1, blocking collectives, local(): lax.all_gather(k_wide, 'frame', axis=0, tiled=True)  7.53 us
    all_to_all x1, starting transfers between devices, local(): lax.all_to_all(keys_in, 'within', split_axis=2, concat_axis=1, tiled=True)  7.31 us
    convert_element_type x1, other arithmetic, grads(): dscore_low = dscore.astype(jnp.bfloat16)  7 us
    another operation x6, local copies, waits for them, and re-layouts  6.93 us
  transfers between devices with their start and end apart: 9, of which 5 were waited for; matrix products, arithmetic and copies ran while one was open for 26% of the time, Pallas kernels for 0%

commit v1 on v0

--- a/solution.py
+++ b/solution.py
@@ -6,12 +6,19 @@
 DH = 64
 
 
+def trade_parts(array, name, split, join):
+    size = lax.axis_size(name)
+    parts = jnp.stack(jnp.split(array, size, axis=split), axis=0)
+    parts = lax.all_to_all(parts, name, split_axis=0, concat_axis=0)
+    return jnp.concatenate(parts, axis=join)
+
+
 def local(queries, keys_in, values_in, grad_out, partners, registers):
     q_wide, k_wide, v_wide, d_wide = (
         lax.all_to_all(queries, "within", split_axis=2, concat_axis=1, tiled=True),
         lax.all_to_all(keys_in, "within", split_axis=2, concat_axis=1, tiled=True),
         lax.all_to_all(values_in, "within", split_axis=2, concat_axis=1, tiled=True),
-        lax.all_to_all(grad_out, "within", split_axis=2, concat_axis=1, tiled=True),
+        trade_parts(grad_out, "within", 2, 1),
     )
     seq = q_wide.shape[1]
     cols = q_wide.shape[2]

time: 194 us -> 200 us (1.031)
  local copies, waits for them, and re-layouts: 38.9 us -> 46.6 us
  other arithmetic: 34.3 us -> 32.3 us
    unnamed x68 -> x67, local copies, waits for them, and re-layouts: 17.3 us -> 24.1 us
    unnamed x7 -> x6, other arithmetic: 14.1 us -> 11.8 us
    another operation x6 -> x7, local copies, waits for them, and re-layouts: 6.93 us -> 8.27 us
  transfers between devices with their start and end apart: 9 -> 9, of which waited for: 5 -> 6; matrix products, arithmetic and copies ran while one was open for 26% -> 29% of each run, Pallas kernels for 0% -> 0%
where the time goes in v1:
time: 200 us; the launch traced here: 198 us
  local copies, waits for them, and re-layouts  46.6 us (23%)
  starting transfers between devices  45.6 us (23%)
  other arithmetic  32.3 us (16%)
  waiting for transfers between devices  32 us (16%)
  matrix products  21.3 us (11%)
  blocking collectives  15.2 us (8%)
  between operations  4.82 us (2%)
    unnamed x67, local copies, waits for them, and re-layouts  24.1 us
    all_to_all x1, waiting for transfers between devices, local(): lax.all_to_all(results[1], 'frame', split_axis=0, concat_axis=0, tiled=True)  11.9 us
    unnamed x6, other arithmetic  11.8 us
    all_gather x1, blocking collectives, local(): lax.all_gather(v_wide, 'frame', axis=0, tiled=True)  7.64 us
    all_gather x1, blocking collectives, local(): lax.all_gather(k_wide, 'frame', axis=0, tiled=True)  7.53 us
    all_to_all x1, starting transfers between devices, local(): lax.all_to_all(keys_in, 'within', split_axis=2, concat_axis=1, tiled=True)  7.31 us
    convert_element_type x1, other arithmetic, grads(): dscore_low = dscore.astype(jnp.bfloat16)  7 us
    another operation x6, local copies, waits for them, and re-layouts  6.93 us
  transfers between devices with their start and end apart: 9, of which 6 were waited for; matrix products, arithmetic and copies ran while one was open for 29% of the time, Pallas kernels for 0%

profile of v1, /device:TPU:0, one launch (start us, length us, event | category | flops | bytes accessed | tf_op | source)
XLA Modules:
  0.0 197.8 jit_solution(6116029653867502488)
XLA Ops:
  2.5 2.4 %reduce.31 = bf16[1024,72]{1,0:T(8,128)(2,1)S(1)} reduce(bf16[1024,1,72]{2,1,0:T(2,128)(2,1)S(1)} %bitcast.202, bf16[]{:T(256)} %broadcast.254), dimensions={1}, to_apply=%bitcast.157.reduce_sub_computation | reduce | bytes 294914
  6.0 7.3 %all-to-all-start.1 = ((bf16[8,2,4608]{2,1,0:T(2,128)(2,1)}), bf16[8,2,4608]{2,1,0:T(2,128)(2,1)S(1)}, u32[]{:S(2)}, u32[]{:S(2)}) async-start(bf16[8,2,4608]{2,1,0:T(2,128)(2,1)} %reshape.379), calls=%async_computation.1 | async-start | bytes 294912 | tf_op jit(solution)/shard_map/all_to_all | solution.py:19
  29.6 2.4 %reduce.30 = bf16[1024,72]{1,0:T(8,128)(2,1)S(1)} reduce(bf16[1024,1,72]{2,1,0:T(2,128)(2,1)S(1)} %bitcast.206, bf16[]{:T(256)} %broadcast.254), dimensions={1}, to_apply=%bitcast.159.reduce_sub_computation | reduce | bytes 294914
  35.1 6.0 %all-to-all-start.3 = ((bf16[8,2,4608]{2,1,0:T(2,128)(2,1)}), bf16[8,2,4608]{2,1,0:T(2,128)(2,1)S(1)}, u32[]{:S(2)}, u32[]{:S(2)}) async-start(bf16[8,2,4608]{2,1,0:T(2,128)(2,1)} %reshape.381), calls=%async_computation.3 | async-start | bytes 294912 | tf_op jit(solution)/shard_map/all_to_all | solution.py:20
  42.8 2.4 %reduce.32 = bf16[1024,72]{1,0:T(8,128)(2,1)S(1)} reduce(bf16[1024,1,72]{2,1,0:T(2,128)(2,1)S(1)} %bitcast.207, bf16[]{:T(256)} %broadcast.254), dimensions={1}, to_apply=%bitcast.161.reduce_sub_computation | reduce | bytes 294914
  48.6 5.1 %all-to-all-start = ((bf16[8,2,4608]{2,1,0:T(2,128)(2,1)}), bf16[8,2,4608]{2,1,0:T(2,128)(2,1)S(1)}, u32[]{:S(2)}, u32[]{:S(2)}) async-start(bf16[8,2,4608]{2,1,0:T(2,128)(2,1)} %reshape.383), calls=%async_computation | async-start | bytes 294912 | tf_op jit(solution)/shard_map/all_to_all | solution.py:18
  55.0 7.5 %all_gather.6 = bf16[4,576,128]{2,1,0:T(8,128)(2,1)S(1)} all-gather(bf16[1,576,128]{2,1,0:T(8,128)(2,1)S(1)} %bitcast.232), channel_id=1, replica_groups=mesh['frame'=4,'within'=8] {'frame'}, dimensions={0}, use_global_device_ids=true | all-gather | bytes 737280 | tf_op jit(solution)/shard_map/all_gather | solution.py:91
  62.5 7.6 %all_gather.7 = bf16[4,576,128]{2,1,0:T(8,128)(2,1)S(1)} all-gather(bf16[1,576,128]{2,1,0:T(8,128)(2,1)S(1)} %bitcast.236), channel_id=1, replica_groups=mesh['frame'=4,'within'=8] {'frame'}, dimensions={0}, use_global_device_ids=true | all-gather | bytes 737280 | tf_op jit(solution)/shard_map/all_gather | solution.py:92
  70.2 6.0 %all-to-all-start.2 = ((bf16[8,1,72,128]{3,2,1,0:T(8,128)(2,1)}), bf16[8,1,72,128]{3,2,1,0:T(8,128)(2,1)S(1)}, u32[]{:S(2)}, u32[]{:S(2)}) async-start(bf16[8,1,72,128]{3,2,1,0:T(8,128)(2,1)} %constant_dynamic-update-slice_fusion), calls=%async_computation.2 | async-start | bytes 294912 | tf_op jit(solution)/shard_map/all_to_all | solution.py:12
  80.0 3.9 %all-to-all-done.2 = bf16[8,1,72,128]{3,2,1,0:T(8,128)(2,1)S(1)} async-done(((bf16[8,1,72,128]{3,2,1,0:T(8,128)(2,1)}), bf16[8,1,72,128]{3,2,1,0:T(8,128)(2,1)S(1)}, u32[]{:S(2)}, u32[]{:S(2)}) %all-to-all-start.2) | async-done | bytes 147488 | tf_op jit(solution)/shard_map/all_to_all | solution.py:12
  90.8 2.7 %fusion.8 = (f32[2,576]{1,0:T(2,128)S(1)}, f32[2,576]{1,0:T(2,128)S(1)}, f32[2,576,576]{1,2,0:T(8,128)}) fusion(f32[2,576,576]{2,1,0:T(8,128)S(1)} %get-tuple-element.99, f32[2,576]{1,0:T(2,128)S(1)} %get-tuple-element.98, pred[576]{0:T(1024)(128)(4,1)S(1)} %get-tuple-element.109, bf16[576,2,64]{0,2,1:T(8,128)(2,1)S(1)} %copy.155, ...), kind=kOutput, calls=%fused_computation.24 | convolution fusion | flops 88913664 | bytes 5617728 | tf_op jit(solution)/shard_map/qhd,khd->hqk/dot_general | solution.py:56
  93.6 2.7 %fusion.7 = (f32[2,576]{1,0:T(2,128)S(1)}, f32[2,576]{1,0:T(2,128)S(1)}, f32[2,576,576]{1,2,0:T(8,128)}) fusion(f32[2,576,576]{2,1,0:T(8,128)S(1)} %get-tuple-element.102, f32[2,576]{1,0:T(2,128)S(1)} %get-tuple-element.101, pred[576]{0:T(1024)(128)(4,1)S(1)} %get-tuple-element.110, bf16[576,2,64]{0,2,1:T(8,128)(2,1)S(1)} %copy.155, ...), kind=kOutput, calls=%fused_computation.23 | convolution fusion | flops 88913664 | bytes 5617728 | tf_op jit(solution)/shard_map/qhd,khd->hqk/dot_general | solution.py:56
  96.3 2.5 %fusion.6 = (f32[2,576]{1,0:T(2,128)S(1)}, f32[2,576]{1,0:T(2,128)S(1)}, f32[2,576,576]{1,2,0:T(8,128)}) fusion(f32[2,576,576]{1,2,0:T(8,128)S(1)} %get-tuple-element.105, f32[2,576]{1,0:T(2,128)S(1)} %get-tuple-element.104, bf16[576,2,64]{0,2,1:T(8,128)(2,1)S(1)} %copy.155, bf16[576,2,64]{0,2,1:T(8,128)(2,1)S(1)} %copy-done.14), kind=kOutput, calls=%fused_computation.22 | convolution fusion | flops 88250112 | bytes 5617152 | tf_op jit(solution)/shard_map/qhd,khd->hqk/dot_general | solution.py:72
  100.5 1.7 fusion.11
  102.2 1.8 copy.142
  104.1 1.8 copy.140
  105.9 2.1 %fusion.21 = f32[2,64,576]{2,1,0:T(8,128)} fusion(bf16[576,2,64]{0,2,1:T(8,128)(2,1)S(1)} %copy.155, f32[2,576,576]{1,2,0:T(8,128)S(1)} %get-tuple-element.105, f32[2,576]{1,0:T(2,128)S(1)} %get-tuple-element.87, f32[2,576]{1,0:T(2,128)S(1)} %get-tuple-element.92, pred[]{:T(512)} %get-tuple-element.95), kind=kOutput, calls=%fused_computation.44 | convolution fusion | flops 87662592 | bytes 3105793 | tf_op jit(solution)/shard_map/hqk,qhd->khd/dot_general | solution.py:83
  107.9 1.8 copy.138
  109.8 7.0 %multiply_convert_fusion.1 = (bf16[2,576,576]{1,2,0:T(8,128)(2,1)S(1)}, bf16[2,576,576]{1,2,0:T(8,128)(2,1)S(1)}, bf16[2,576,576]{1,2,0:T(8,128)(2,1)S(1)}) fusion(f32[2,576,576]{1,2,0:T(8,128)} %get-tuple-element.103, f32[2,576]{1,0:T(2,128)S(1)} %get-tuple-element.88, f32[2,576]{1,0:T(2,128)S(1)} %get-tuple-element.87, f32[2,576]{1,0:T(2,128)S(1)} %get-tuple-element.92, ...), kind=kLoop, calls=%fused_computation.13 | loop fusion | flops 13271040 | bytes 19921536 | tf_op jit(solution)/shard_map/convert_element_type | solution.py:74
  121.4 4.0 %all-to-all-start.4 = ((bf16[8,2,4608]{2,1,0:T(2,128)(2,1)}), bf16[8,2,4608]{2,1,0:T(2,128)(2,1)}, u32[]{:S(2)}, u32[]{:S(2)}) async-start(bf16[8,2,4608]{2,1,0:T(2,128)(2,1)} %reshape.385), calls=%async_computation.4 | async-start | bytes 294912 | tf_op jit(solution)/shard_map/all_to_all | solution.py:125
  127.2 2.5 %fusion.27 = f32[4,576,128]{2,1,0:T(8,128)} fusion(f32[4,576,128]{2,1,0:T(8,128)} %constant_dynamic-update-slice_fusion.8, s32[]{:T(128)} %select_n.49, f32[1,576,128]{2,1,0:T(8,128)} %copy.140, pred[]{:T(512)} %get-tuple-element.82), kind=kLoop, calls=%fused_computation.52 | loop fusion | flops 147456 | bytes 885760 | tf_op jit(solution)/shard_map/scatter-add | solution.py:112
  129.7 2.3 %fusion.28 = f32[4,576,128]{2,1,0:T(8,128)} fusion(f32[4,576,128]{2,1,0:T(8,128)} %fusion.27, s32[]{:T(128)} %select_n.52, f32[1,576,128]{2,1,0:T(8,128)S(1)} %copy-done.12, pred[]{:T(512)} %get-tuple-element.81), kind=kLoop, calls=%fused_computation.53 | loop fusion | flops 147456 | bytes 885760 | tf_op jit(solution)/shard_map/scatter-add | solution.py:112
  133.2 4.4 %all-to-all-start.7 = ((f32[4,576,128]{2,1,0:T(8,128)}), f32[4,576,128]{2,1,0:T(8,128)}, u32[]{:S(2)}, u32[]{:S(2)}) async-start(f32[4,576,128]{2,1,0:T(8,128)} %fusion.28), calls=%async_computation.7 | async-start | bytes 2359296 | tf_op jit(solution)/shard_map/all_to_all | solution.py:117
  142.7 2.3 %fusion.25 = f32[4,576,128]{2,1,0:T(8,128)} fusion(f32[4,576,128]{2,1,0:T(8,128)} %constant_dynamic-update-slice_fusion.9, s32[]{:T(128)} %select_n.49, f32[1,576,128]{2,1,0:T(8,128)S(1)} %copy.131, pred[]{:T(512)} %get-tuple-element.82), kind=kLoop, calls=%fused_computation.50 | loop fusion | flops 147456 | bytes 885760 | tf_op jit(solution)/shard_map/scatter-add | solution.py:111
  145.0 2.3 %fusion.26 = f32[4,576,128]{2,1,0:T(8,128)} fusion(f32[4,576,128]{2,1,0:T(8,128)} %fusion.25, s32[]{:T(128)} %select_n.52, f32[1,576,128]{2,1,0:T(8,128)S(1)} %copy.133, pred[]{:T(512)} %get-tuple-element.81), kind=kLoop, calls=%fused_computation.51 | loop fusion | flops 147456 | bytes 885760 | tf_op jit(solution)/shard_map/scatter-add | solution.py:111
  147.3 6.2 %all-to-all-done.7 = f32[4,576,128]{2,1,0:T(8,128)} async-done(((f32[4,576,128]{2,1,0:T(8,128)}), f32[4,576,128]{2,1,0:T(8,128)}, u32[]{:S(2)}, u32[]{:S(2)}) %all-to-all-start.7) | async-done | bytes 1179680 | tf_op jit(solution)/shard_map/all_to_all | solution.py:117
  153.5 3.5 %all-to-all-start.5 = ((f32[4,576,128]{2,1,0:T(8,128)}), f32[4,576,128]{2,1,0:T(8,128)S(1)}, u32[]{:S(2)}, u32[]{:S(2)}) async-start(f32[4,576,128]{2,1,0:T(8,128)} %fusion.26), calls=%async_computation.5 | async-start | bytes 2359296 | tf_op jit(solution)/shard_map/all_to_all | solution.py:116
  161.0 11.9 %all-to-all-done.5 = f32[4,576,128]{2,1,0:T(8,128)S(1)} async-done(((f32[4,576,128]{2,1,0:T(8,128)}), f32[4,576,128]{2,1,0:T(8,128)S(1)}, u32[]{:S(2)}, u32[]{:S(2)}) %all-to-all-start.5) | async-done | bytes 1179680 | tf_op jit(solution)/shard_map/all_to_all | solution.py:116
  172.8 5.9 %all-to-all-start.8 = ((bf16[8,2,4608]{2,1,0:T(2,128)(2,1)}), bf16[8,2,4608]{2,1,0:T(2,128)(2,1)S(1)}, u32[]{:S(2)}, u32[]{:S(2)}) async-start(bf16[8,2,4608]{2,1,0:T(2,128)(2,1)} %reshape.389), calls=%async_computation.8 | async-start | bytes 294912 | tf_op jit(solution)/shard_map/all_to_all | solution.py:127
  181.4 4.8 %all-to-all-done.8 = bf16[8,2,4608]{2,1,0:T(2,128)(2,1)S(1)} async-done(((bf16[8,2,4608]{2,1,0:T(2,128)(2,1)}), bf16[8,2,4608]{2,1,0:T(2,128)(2,1)S(1)}, u32[]{:S(2)}, u32[]{:S(2)}) %all-to-all-start.8) | async-done | bytes 147488 | tf_op jit(solution)/shard_map/all_to_all | solution.py:127
  186.2 3.4 %all-to-all-start.6 = ((bf16[8,2,4608]{2,1,0:T(2,128)(2,1)}), bf16[8,2,4608]{2,1,0:T(2,128)(2,1)S(1)}, u32[]{:S(2)}, u32[]{:S(2)}) async-start(bf16[8,2,4608]{2,1,0:T(2,128)(2,1)} %reshape.387), calls=%async_computation.6 | async-start | bytes 294912 | tf_op jit(solution)/shard_map/all_to_all | solution.py:126
  192.6 4.4 %all-to-all-done.6 = bf16[8,2,4608]{2,1,0:T(2,128)(2,1)S(1)} async-done(((bf16[8,2,4608]{2,1,0:T(2,128)(2,1)}), bf16[8,2,4608]{2,1,0:T(2,128)(2,1)S(1)}, u32[]{:S(2)}, u32[]{:S(2)}) %all-to-all-start.6) | async-done | bytes 147488 | tf_op jit(solution)/shard_map/all_to_all | solution.py:126
  (127 shorter events, 60.3 us)
Async XLA Ops:
  0.6 12.7 %copy-start = (s32[4,2]{0,1:T(2,128)S(1)}, s32[4,2]{0,1:T(2,128)}, u32[]{:S(2)}) copy-start(s32[4,2]{0,1:T(2,128)} %param.22) | copy-start | bytes 100
  0.6 32.5 %copy-start.17 = (s32[4]{0:T(128)S(1)}, s32[4]{0:T(128)}, u32[]{:S(2)}) copy-start(s32[4]{0:T(128)} %param.23) | copy-start | bytes 52
  0.7 41.7 %copy-start.16 = (bf16[1,72,1024]{2,1,0:T(8,128)(2,1)S(1)}, bf16[1,72,1024]{2,1,0:T(8,128)(2,1)}, u32[]{:S(2)}) copy-start(bf16[1,72,1024]{2,1,0:T(8,128)(2,1)} %param.18) | copy-start | bytes 442372
  6.0 29.1 %all-to-all-start.1 = ((bf16[8,2,4608]{2,1,0:T(2,128)(2,1)}), bf16[8,2,4608]{2,1,0:T(2,128)(2,1)S(1)}, u32[]{:S(2)}, u32[]{:S(2)}) async-start(bf16[8,2,4608]{2,1,0:T(2,128)(2,1)} %reshape.379), calls=%async_computation.1 | async-start | bytes 294912 | tf_op jit(solution)/shard_map/all_to_all | solution.py:19
  35.1 13.4 %all-to-all-start.3 = ((bf16[8,2,4608]{2,1,0:T(2,128)(2,1)}), bf16[8,2,4608]{2,1,0:T(2,128)(2,1)S(1)}, u32[]{:S(2)}, u32[]{:S(2)}) async-start(bf16[8,2,4608]{2,1,0:T(2,128)(2,1)} %reshape.381), calls=%async_computation.3 | async-start | bytes 294912 | tf_op jit(solution)/shard_map/all_to_all | solution.py:20
  48.6 21.6 %all-to-all-start = ((bf16[8,2,4608]{2,1,0:T(2,128)(2,1)}), bf16[8,2,4608]{2,1,0:T(2,128)(2,1)S(1)}, u32[]{:S(2)}, u32[]{:S(2)}) async-start(bf16[8,2,4608]{2,1,0:T(2,128)(2,1)} %reshape.383), calls=%async_computation | async-start | bytes 294912 | tf_op jit(solution)/shard_map/all_to_all | solution.py:18
  70.2 13.7 %all-to-all-start.2 = ((bf16[8,1,72,128]{3,2,1,0:T(8,128)(2,1)}), bf16[8,1,72,128]{3,2,1,0:T(8,128)(2,1)S(1)}, u32[]{:S(2)}, u32[]{:S(2)}) async-start(bf16[8,1,72,128]{3,2,1,0:T(8,128)(2,1)} %constant_dynamic-update-slice_fusion), calls=%async_computation.2 | async-start | bytes 294912 | tf_op jit(solution)/shard_map/all_to_all | solution.py:12
  88.5 2.3 %copy-start.13 = (bf16[1,576,128]{1,2,0:T(8,128)(2,1)S(1)}, bf16[1,576,128]{1,2,0:T(8,128)(2,1)}, u32[]{:S(2)}) copy-start(bf16[1,576,128]{1,2,0:T(8,128)(2,1)} %copy.122) | copy-start | bytes 442372
  90.1 8.7 %copy-start.1 = (f32[2,576,576]{2,1,0:T(8,128)}, f32[2,576,576]{2,1,0:T(8,128)S(1)}, u32[]{:S(2)}) copy-start(f32[2,576,576]{2,1,0:T(8,128)S(1)} %get-tuple-element.99) | copy-start | bytes 7962628
  90.8 9.7 %copy-start.2 = (f32[2,576,576]{2,1,0:T(8,128)}, f32[2,576,576]{2,1,0:T(8,128)S(1)}, u32[]{:S(2)}) copy-start(f32[2,576,576]{2,1,0:T(8,128)S(1)} %get-tuple-element.102) | copy-start | bytes 7962628
  90.8 2.7 %copy-start.15 = (bf16[1,576,128]{1,2,0:T(8,128)(2,1)S(1)}, bf16[1,576,128]{1,2,0:T(8,128)(2,1)}, u32[]{:S(2)}) copy-start(bf16[1,576,128]{1,2,0:T(8,128)(2,1)} %copy.121) | copy-start | bytes 442372
  93.6 2.7 %copy-start.14 = (bf16[576,2,64]{0,2,1:T(8,128)(2,1)S(1)}, bf16[576,2,64]{0,2,1:T(8,128)(2,1)}, u32[]{:S(2)}) copy-start(bf16[576,2,64]{0,2,1:T(8,128)(2,1)} %reshape_squeeze.29) | copy-start | bytes 442372
  109.8 7.0 %copy-start.10 = (bf16[576,2,64]{0,2,1:T(8,128)(2,1)S(1)}, bf16[576,2,64]{0,2,1:T(8,128)(2,1)}, u32[]{:S(2)}) copy-start(bf16[576,2,64]{0,2,1:T(8,128)(2,1)} %reshape_squeeze.26) | copy-start | bytes 442372
  109.8 7.4 %copy-start.9 = (bf16[1,576,128]{1,2,0:T(8,128)(2,1)S(1)}, bf16[1,576,128]{1,2,0:T(8,128)(2,1)}, u32[]{:S(2)}) copy-start(bf16[1,576,128]{1,2,0:T(8,128)(2,1)} %copy.115) | copy-start | bytes 442372
  116.8 1.2 copy-start.3
  116.8 1.6 copy-start.5
  116.8 2.0 %copy-start.7 = (bf16[2,576,576]{1,2,0:T(8,128)(2,1)}, bf16[2,576,576]{1,2,0:T(8,128)(2,1)S(1)}, u32[]{:S(2)}) copy-start(bf16[2,576,576]{1,2,0:T(8,128)(2,1)S(1)} %get-tuple-element.91) | copy-start | bytes 3981316
  117.6 8.8 %copy-start.11 = (f32[1,576,128]{2,1,0:T(8,128)S(1)}, f32[1,576,128]{2,1,0:T(8,128)}, u32[]{:S(2)}) copy-start(f32[1,576,128]{2,1,0:T(8,128)} %copy.138) | copy-start | bytes 884740
  118.8 10.9 %copy-start.12 = (f32[1,576,128]{2,1,0:T(8,128)S(1)}, f32[1,576,128]{2,1,0:T(8,128)}, u32[]{:S(2)}) copy-start(f32[1,576,128]{2,1,0:T(8,128)} %copy.142) | copy-start | bytes 884740
  118.8 13.2 %copy-start.8 = (bf16[2,576,576]{1,2,0:T(8,128)(2,1)S(1)}, bf16[2,576,576]{1,2,0:T(8,128)(2,1)}, u32[]{:S(2)}) copy-start(bf16[2,576,576]{1,2,0:T(8,128)(2,1)} %copy-done.7) | copy-start | bytes 3981316
  121.4 11.8 %all-to-all-start.4 = ((bf16[8,2,4608]{2,1,0:T(2,128)(2,1)}), bf16[8,2,4608]{2,1,0:T(2,128)(2,1)}, u32[]{:S(2)}, u32[]{:S(2)}) async-start(bf16[8,2,4608]{2,1,0:T(2,128)(2,1)} %reshape.385), calls=%async_computation.4 | async-start | bytes 294912 | tf_op jit(solution)/shard_map/all_to_all | solution.py:125
  127.2 10.4 %copy-start.4 = (bf16[2,576,576]{1,2,0:T(8,128)(2,1)S(1)}, bf16[2,576,576]{1,2,0:T(8,128)(2,1)}, u32[]{:S(2)}) copy-start(bf16[2,576,576]{1,2,0:T(8,128)(2,1)} %copy-done.3) | copy-start | bytes 3981316
  133.1 7.0 %copy-start.6 = (bf16[2,576,576]{1,2,0:T(8,128)(2,1)S(1)}, bf16[2,576,576]{1,2,0:T(8,128)(2,1)}, u32[]{:S(2)}) copy-start(bf16[2,576,576]{1,2,0:T(8,128)(2,1)} %copy-done.5) | copy-start | bytes 3981316
  133.2 20.3 %all-to-all-start.7 = ((f32[4,576,128]{2,1,0:T(8,128)}), f32[4,576,128]{2,1,0:T(8,128)}, u32[]{:S(2)}, u32[]{:S(2)}) async-start(f32[4,576,128]{2,1,0:T(8,128)} %fusion.28), calls=%async_computation.7 | async-start | bytes 2359296 | tf_op jit(solution)/shard_map/all_to_all | solution.py:117
  153.5 19.3 %all-to-all-start.5 = ((f32[4,576,128]{2,1,0:T(8,128)}), f32[4,576,128]{2,1,0:T(8,128)S(1)}, u32[]{:S(2)}, u32[]{:S(2)}) async-start(f32[4,576,128]{2,1,0:T(8,128)} %fusion.26), calls=%async_computation.5 | async-start | bytes 2359296 | tf_op jit(solution)/shard_map/all_to_all | solution.py:116
  172.8 13.4 %all-to-all-start.8 = ((bf16[8,2,4608]{2,1,0:T(2,128)(2,1)}), bf16[8,2,4608]{2,1,0:T(2,128)(2,1)S(1)}, u32[]{:S(2)}, u32[]{:S(2)}) async-start(bf16[8,2,4608]{2,1,0:T(2,128)(2,1)} %reshape.389), calls=%async_computation.8 | async-start | bytes 294912 | tf_op jit(solution)/shard_map/all_to_all | solution.py:127
  186.2 10.8 %all-to-all-start.6 = ((bf16[8,2,4608]{2,1,0:T(2,128)(2,1)}), bf16[8,2,4608]{2,1,0:T(2,128)(2,1)S(1)}, u32[]{:S(2)}, u32[]{:S(2)}) async-start(bf16[8,2,4608]{2,1,0:T(2,128)(2,1)} %reshape.387), calls=%async_computation.6 | async-start | bytes 294912 | tf_op jit(solution)/shard_map/all_to_all | solution.py:126
